TPU v7x, 32 devices: a whole 2x2x4 slice. The times are simulated.
32 devices in a mesh: seq: 8 (over z, y), tp: 4 (over x, core).
Axes of the slice: x: 2, y: 2, z: 4, core: 2. Of those that a mesh axis runs over, the one named last changes fastest.
Arguments:
- tokens: bfloat16 [6144, 2048], P('seq', 'tp'), may hold values from -20 to 20
- w_query: bfloat16 [2048, 2048], P(None, 'tp'), may hold values from -0.125 to 0.125
- w_key: bfloat16 [2048, 2048], P(None, 'tp'), may hold values from -0.125 to 0.125
- w_value: bfloat16 [2048, 2048], P(None, 'tp'), may hold values from -0.125 to 0.125
- head_gain: float32 [2048], P('tp'), may hold values from 0.5 to 1.5
- w_out: bfloat16 [2048, 2048], P('tp'), may hold values from -0.125 to 0.125
- norm_gain: float32 [2048], replicated, may hold values from 0.5 to 1.5
- w_gate: bfloat16 [2048, 8192], P('seq', 'tp'), may hold values from -0.125 to 0.125
- w_up: bfloat16 [2048, 8192], P('seq', 'tp'), may hold values from -0.125 to 0.125
- w_down: bfloat16 [8192, 2048], P('tp', 'seq'), may hold values from -0.0625 to 0.0625
Outputs:
- layer_out: bfloat16 [6144, 2048], P('seq', 'tp')
All inputs are finite; a program needn't handle non-finite values.
Results may differ from a plain program's by a relative error of at most 0.009.
Values may be sent and summed in bfloat16 or wider, within the bound.
A program may use at most 128 MiB of HBM per device.

v0:
```python
import jax
import jax.numpy as jnp
from jax import lax
from jax.experimental.layout import Layout, with_layout_constraint
from jax.sharding import PartitionSpec as P

HD = 128
F32 = jnp.float32
BF16 = jnp.bfloat16


def make_body(n_seq, n_tp):
    pair = n_seq // 2
    seq_bits = [1 << b for b in range(n_seq.bit_length() - 1)]
    tp_bits = [1 << b for b in range(n_tp.bit_length() - 1)]
    spread_bits = [b for b in reversed(seq_bits) if b != pair]

    def swap(value, axis, bit):
        size = n_seq if axis == "seq" else n_tp
        return lax.ppermute(value, axis, [(i, i ^ bit) for i in range(size)])

    def spread(held, axis, bits):
        held = dict(held)
        for bit in bits:
            held.update({r ^ bit: swap(v, axis, bit) for r, v in held.items()})
        return held

    def gather_tp(value):
        return spread({0: value}, "tp", list(reversed(tp_bits)))

    def scatter_tp(terms):
        terms = dict(terms)
        for bit in tp_bits:
            for r in [r for r in terms if r & bit]:
                moved = swap(terms.pop(r).astype(BF16), "tp", bit)
                terms[r ^ bit] = terms[r ^ bit] + moved.astype(F32)
        return terms[0]

    def body(tokens, w_query, w_key, w_value, head_gain, w_out, norm_gain, w_gate, w_up, w_down):
        length, width = tokens.shape
        heads = w_query.shape[1] // HD
        model = norm_gain.shape[0]
        me_seq = lax.axis_index("seq")
        me_tp = lax.axis_index("tp")
        part = ((me_seq & pair) != 0).astype(jnp.int32)
        half = w_gate.shape[1] // 2
        rows = w_gate.shape[0]

        def halves(weight, dim):
            keep = lax.dynamic_slice_in_dim(weight, part * half, half, dim)
            give = lax.dynamic_slice_in_dim(weight, (1 - part) * half, half, dim)
            return keep, give

        def assemble(pieces, dim):
            shape = list(pieces[0].shape)
            shape[dim] = n_seq * rows
            out = jnp.zeros(shape, BF16)
            for r, piece in pieces.items():
                out = lax.dynamic_update_slice_in_dim(out, piece, (me_seq ^ r) * rows, dim)
            return out

        def after(values, anchor):
            keys_of = list(values)
            out = lax.optimization_barrier(tuple(values[k] for k in keys_of) + (anchor,))
            return dict(zip(keys_of, out[:-1])), out[-1]

        def hops(pieces, bits):
            return {r ^ bit: swap(v, "seq", bit) for bit in bits for r, v in pieces.items()}

        def matmul(a, b):
            return jnp.dot(a, b, preferred_element_type=F32)

        def side_by_side(pieces):
            out = jnp.zeros((length, model), BF16)
            for r in sorted(pieces):
                out = lax.dynamic_update_slice_in_dim(out, pieces[r], (me_tp ^ r) * width, 1)
            return out

        def to_features(value, weight):
            terms = {}
            for r in reversed(range(n_tp)):
                block = lax.dynamic_slice_in_dim(weight, (me_tp ^ r) * width, width, 1)
                terms[r] = matmul(value, block)
            return scatter_tp(terms)

        first, last = spread_bits[:-1], spread_bits[-1:]
        gate_keep, gate_give = halves(w_gate, 1)
        up_keep, up_give = halves(w_up, 1)
        down_keep, down_give = halves(w_down, 0)
        wide_own = {0: jnp.concatenate([gate_keep, up_keep], axis=1)}
        wide_give = jnp.concatenate([gate_give, up_give], axis=1)
        tall_own = {0: down_keep}

        features = with_layout_constraint(side_by_side(gather_tp(tokens)), Layout((0, 1)))
        wide_got = {pair: swap(wide_give, "seq", pair)}
        wide_far = dict(wide_own)
        for bit in first:
            wide_far.update(hops(wide_far, [bit]))
        wide_near = hops(wide_own, last)
        tall_far = dict(tall_own)
        for bit in first:
            tall_far.update(hops(tall_far, [bit]))
        tall_near = hops(tall_own, last)

        def project(weight):
            return matmul(features, weight).astype(BF16).reshape(length, heads, HD)

        keys = project(w_key)
        values = project(w_value)
        state = jnp.einsum("jhd,jhe->hde", keys, values, preferred_element_type=F32)
        query = project(w_query)
        history = jnp.zeros_like(state)
        total = state
        for bit in seq_bits:
            other = swap(total.astype(BF16), "seq", bit).astype(F32)
            history = history + jnp.where((me_seq & bit) != 0, other, 0.0)
            total = total + other
            if bit in last:
                wide_far, total = after(wide_far, total)
        history = history.astype(BF16)
        (tall_give, history) = after({pair: down_give}, history)
        wide_got, history = after(wide_got, history)
        tall_got = {pair: swap(tall_give[pair], "seq", pair)}
        for bit in first:
            wide_got.update(hops(wide_got, [bit]))
        near = {**wide_near, **hops({r: v for r, v in wide_far.items() if r}, last)}
        wide = {**wide_far, **near}
        scores = jnp.einsum("ihd,jhd->hij", query, keys, preferred_element_type=F32)
        causal = jnp.arange(length)[:, None] >= jnp.arange(length)[None, :]
        scores = jnp.where(causal[None], scores, 0.0).astype(BF16)
        inside = jnp.einsum("hij,jhd->ihd", scores, values, preferred_element_type=F32)
        wide_got.update(hops(wide_got, last))
        wide.update(wide_got)
        carried = jnp.einsum(
            "ihd,hde->ihe", query, history, preferred_element_type=F32
        )
        mixed = inside + carried
        scale = lax.rsqrt(jnp.mean(mixed * mixed, axis=-1, keepdims=True) + 1e-06)
        normed = (mixed * scale * head_gain.reshape(heads, HD)).astype(BF16)
        normed = normed.reshape(length, heads * HD)
        resid = tokens.astype(F32) + to_features(normed, w_out)
        gain = lax.dynamic_slice_in_dim(norm_gain, me_tp * width, width, 0)
        own_in = (resid * gain).astype(BF16)
        pair_in = swap(own_in, "seq", pair)
        own_pieces = gather_tp(own_in)
        pair_pieces = gather_tp(pair_in)
        tall_far, own_in = after({r: v for r, v in tall_far.items() if r}, own_in)
        tall_got, own_in = after(tall_got, own_in)
        tall = {**tall_own, **tall_near, **tall_far, **hops(tall_far, last)}
        for bit in first:
            tall_got.update(hops(tall_got, [bit]))
        tall_got.update(hops(tall_got, last))
        tall.update(tall_got)
        squares = jnp.sum(resid * resid, axis=-1)
        for bit in tp_bits:
            squares = squares + swap(squares, "tp", bit)
        pair_squares = swap(squares, "seq", pair)
        wide_whole = assemble(wide, 0)
        gate_whole, up_whole = wide_whole[:, :half], wide_whole[:, half:]
        down_whole = assemble(tall, 1)

        def feed(pieces, total):
            factor = lax.rsqrt(total / model + 1e-05)[:, None]
            ffn_in = side_by_side(pieces)
            gate = matmul(ffn_in, gate_whole) * factor
            upward = matmul(ffn_in, up_whole) * factor
            hidden = (jax.nn.silu(gate) * upward).astype(BF16)
            return to_features(hidden, down_whole)

        pair_out = feed(pair_pieces, pair_squares)
        own_out = feed(own_pieces, squares)
        back = swap(pair_out.astype(BF16), "seq", pair)
        return (resid + own_out + back.astype(F32)).astype(BF16)

    return body


def solution(mesh):
    body = make_body(mesh.shape["seq"], mesh.shape["tp"])

    return jax.shard_map(
        body,
        mesh=mesh,
        in_specs=(
            P("seq", "tp"),
            P(None, "tp"),
            P(None, "tp"),
            P(None, "tp"),
            P("tp"),
            P("tp", None),
            P(),
            P("seq", "tp"),
            P("seq", "tp"),
            P("tp", "seq"),
        ),
        out_specs=P("seq", "tp"),
        check_vma=False,
    )
```

profile of v0, /device:TPU:0, one launch (start us, length us, event | category | flops | bytes accessed | tf_op | source)
XLA Modules:
  0.0 341.2 jit_solution(12053302449331104570)
XLA Ops:
  0.0 3.0 collective-permute-start.1
  3.0 2.7 constant_dynamic-slice_fusion.1
  5.7 15.1 %collective-permute-done.1 = bf16[768,512]{1,0:T(8,128)(2,1)} collective-permute-done((bf16[768,512]{1,0:T(8,128)(2,1)}, bf16[768,512]{1,0:T(8,128)(2,1)}, u32[]{:S(2)}, u32[]{:S(2)}) %collective-permute-start.1) | collective-permute-done | bytes 786464 | tf_op jit(solution)/shard_map/ppermute | solution.py:20
  24.3 2.5 broadcast_in_dim.35
  44.1 18.0 %collective-permute-done.4 = bf16[4,128,128]{2,1,0:T(8,128)(2,1)S(1)} collective-permute-done((bf16[4,128,128]{2,1,0:T(8,128)(2,1)}, bf16[4,128,128]{2,1,0:T(8,128)(2,1)S(1)}, u32[]{:S(2)}, u32[]{:S(2)}) %collective-permute-start.4) | collective-permute-done | bytes 131104 | tf_op jit(solution)/shard_map/ppermute | solution.py:20
  62.1 2.6 collective-permute-start.3
  65.3 5.3 %convolution_convert_fusion.1 = bf16[768,512]{0,1:T(8,128)(2,1)} fusion(bf16[768,2048]{1,0:T(8,128)(2,1)} %copy-done.2, bf16[2048,512]{1,0:T(8,128)(2,1)} %param.11), kind=kOutput, calls=%fused_computation.31 | convolution fusion | flops 1611005952 | bytes 6029312 | tf_op jit(solution)/shard_map/dot_general | solution.py:71
  70.6 19.1 %collective-permute-done.6 = bf16[4,128,128]{2,1,0:T(8,128)(2,1)S(1)} collective-permute-done((bf16[4,128,128]{2,1,0:T(8,128)(2,1)S(1)}, bf16[4,128,128]{2,1,0:T(8,128)(2,1)S(1)}, u32[]{:S(2)}, u32[]{:S(2)}) %collective-permute-start.6) | collective-permute-done | bytes 131104 | tf_op jit(solution)/shard_map/ppermute | solution.py:20
  91.2 5.9 %fusion = f32[4,128,768]{2,1,0:T(8,128)} fusion(bf16[768,4,128]{0,2,1:T(8,128)(2,1)} %bitcast.50, pred[768,768]{1,0:T(8,128)(4,1)} %iota_compare_fusion, bf16[768,4,128]{0,2,1:T(8,128)(2,1)} %bitcast.47, bf16[768,4,128]{0,2,1:T(8,128)(2,1)} %bitcast.52), kind=kOutput, calls=%fused_computation.1 | convolution fusion | flops 1212678144 | bytes 4521984 | tf_op jit(solution)/shard_map/hij,jhd->ihd/dot_general | solution.py:131
  97.0 18.8 %collective-permute-done.7 = bf16[4,128,128]{2,1,0:T(8,128)(2,1)} collective-permute-done((bf16[4,128,128]{2,1,0:T(8,128)(2,1)S(1)}, bf16[4,128,128]{2,1,0:T(8,128)(2,1)}, u32[]{:S(2)}, u32[]{:S(2)}) %collective-permute-start.7) | collective-permute-done | bytes 131104 | tf_op jit(solution)/shard_map/ppermute | solution.py:20
  131.0 22.1 %collective-permute-done.24 = bf16[1024,256]{1,0:T(8,128)(2,1)S(1)} collective-permute-done((bf16[1024,256]{1,0:T(8,128)(2,1)S(1)}, bf16[1024,256]{1,0:T(8,128)(2,1)S(1)}, u32[]{:S(2)}, u32[]{:S(2)}) %collective-permute-start.24) | collective-permute-done | bytes 524320 | tf_op jit(solution)/shard_map/ppermute | solution.py:20
  159.9 19.5 %collective-permute-done.16 = bf16[256,2048]{1,0:T(8,128)(2,1)S(1)} collective-permute-done((bf16[256,2048]{1,0:T(8,128)(2,1)}, bf16[256,2048]{1,0:T(8,128)(2,1)S(1)}, u32[]{:S(2)}, u32[]{:S(2)}) %collective-permute-start.16) | collective-permute-done | bytes 1048608 | tf_op jit(solution)/shard_map/ppermute | solution.py:20
  186.1 6.9 %collective-permute-done.25 = bf16[1024,256]{1,0:T(8,128)(2,1)S(1)} collective-permute-done((bf16[1024,256]{1,0:T(8,128)(2,1)S(1)}, bf16[1024,256]{1,0:T(8,128)(2,1)S(1)}, u32[]{:S(2)}, u32[]{:S(2)}) %collective-permute-start.25) | collective-permute-done | bytes 524320 | tf_op jit(solution)/shard_map/ppermute | solution.py:20
  195.7 24.0 %collective-permute-done.35 = f32[768]{0:T(1024)S(1)} collective-permute-done((f32[768]{0:T(1024)S(1)}, f32[768]{0:T(1024)S(1)}, u32[]{:S(2)}, u32[]{:S(2)}) %collective-permute-start.35) | collective-permute-done | bytes 3104 | tf_op jit(solution)/shard_map/ppermute | solution.py:20
  220.3 4.0 %collective-permute-done.23 = bf16[1024,256]{1,0:T(8,128)(2,1)S(1)} collective-permute-done((bf16[1024,256]{1,0:T(8,128)(2,1)}, bf16[1024,256]{1,0:T(8,128)(2,1)S(1)}, u32[]{:S(2)}, u32[]{:S(2)}) %collective-permute-start.23) | collective-permute-done | bytes 524320 | tf_op jit(solution)/shard_map/ppermute | solution.py:20
  227.4 7.2 %collective-permute-done.27 = bf16[1024,256]{1,0:T(8,128)(2,1)S(1)} collective-permute-done((bf16[1024,256]{1,0:T(8,128)(2,1)S(1)}, bf16[1024,256]{1,0:T(8,128)(2,1)S(1)}, u32[]{:S(2)}, u32[]{:S(2)}) %collective-permute-start.27) | collective-permute-done | bytes 524320 | tf_op jit(solution)/shard_map/ppermute | solution.py:20
  240.4 14.4 %collective-permute-done.33 = bf16[768,512]{1,0:T(8,128)(2,1)S(1)} collective-permute-done((bf16[768,512]{1,0:T(8,128)(2,1)S(1)}, bf16[768,512]{1,0:T(8,128)(2,1)S(1)}, u32[]{:S(2)}, u32[]{:S(2)}) %collective-permute-start.33) | collective-permute-done | bytes 786464 | tf_op jit(solution)/shard_map/ppermute | solution.py:20
  255.1 3.4 %fusion.11 = f32[768,1024]{1,0:T(8,128)S(1)} fusion(bf16[768,2048]{1,0:T(8,128)(2,1)S(1)} %constant_dynamic-update-slice_fusion.20, bf16[2048,2048]{1,0:T(8,128)(2,1)S(1)} %constant_dynamic-update-slice_fusion.12), kind=kOutput, calls=%fused_computation.11 | convolution fusion | flops 3221225472 | bytes 10485760 | tf_op jit(solution)/shard_map/dot_general | solution.py:71
  258.7 3.4 %fusion.9 = f32[768,1024]{1,0:T(8,128)S(1)} fusion(bf16[768,2048]{1,0:T(8,128)(2,1)S(1)} %constant_dynamic-update-slice_fusion, bf16[2048,2048]{1,0:T(8,128)(2,1)S(1)} %constant_dynamic-update-slice_fusion.12), kind=kOutput, calls=%fused_computation.9 | convolution fusion | flops 3221225472 | bytes 10485760 | tf_op jit(solution)/shard_map/dot_general | solution.py:71
  262.1 4.1 %multiply_convert_fusion = bf16[768,1024]{1,0:T(8,128)(2,1)S(1)} fusion(f32[768,1024]{1,0:T(8,128)S(1)} %fusion.9, bf16[768,2048]{1,0:T(8,128)(2,1)S(1)} %constant_dynamic-update-slice_fusion, bf16[2048,2048]{1,0:T(8,128)(2,1)S(1)} %constant_dynamic-update-slice_fusion.12, f32[768]{0:T(1024)S(1)} %add_rsqrt_fusion.1), kind=kOutput, calls=%fused_computation.13 | convolution fusion | flops 3227516928 | bytes 12062720 | tf_op jit(solution)/shard_map/dot_general | solution.py:71
  266.2 2.2 convolution_convert_fusion.3
  269.0 3.9 %multiply_convert_fusion.1 = bf16[768,1024]{1,0:T(8,128)(2,1)S(1)} fusion(f32[768,1024]{1,0:T(8,128)S(1)} %fusion.11, bf16[768,2048]{1,0:T(8,128)(2,1)S(1)} %constant_dynamic-update-slice_fusion.20, bf16[2048,2048]{1,0:T(8,128)(2,1)S(1)} %constant_dynamic-update-slice_fusion.12, f32[768]{0:T(1024)S(1)} %get-tuple-element.21), kind=kOutput, calls=%fused_computation.14 | convolution fusion | flops 3227516928 | bytes 12062720 | tf_op jit(solution)/shard_map/dot_general | solution.py:71
  272.9 2.2 convolution_convert_fusion.5
  275.2 2.2 convolution_convert_fusion.4
  277.9 2.2 add_convert_fusion.2
  280.8 2.2 convolution_convert_fusion.6
  283.1 2.2 add_convert_fusion.3
  286.9 13.8 %collective-permute-done.38 = bf16[768,512]{1,0:T(8,128)(2,1)S(1)} collective-permute-done((bf16[768,512]{1,0:T(8,128)(2,1)S(1)}, bf16[768,512]{1,0:T(8,128)(2,1)S(1)}, u32[]{:S(2)}, u32[]{:S(2)}) %collective-permute-start.38) | collective-permute-done | bytes 786464 | tf_op jit(solution)/shard_map/ppermute | solution.py:20
  300.6 2.4 add_convert_fusion.1
  303.2 13.4 %collective-permute-done.30 = bf16[768,512]{1,0:T(8,128)(2,1)S(1)} collective-permute-done((bf16[768,512]{1,0:T(8,128)(2,1)S(1)}, bf16[768,512]{1,0:T(8,128)(2,1)S(1)}, u32[]{:S(2)}, u32[]{:S(2)}) %collective-permute-start.30) | collective-permute-done | bytes 786464 | tf_op jit(solution)/shard_map/ppermute | solution.py:20
  316.6 21.4 %collective-permute-done.39 = bf16[768,512]{1,0:T(8,128)(2,1)S(1)} collective-permute-done((bf16[768,512]{1,0:T(8,128)(2,1)S(1)}, bf16[768,512]{1,0:T(8,128)(2,1)S(1)}, u32[]{:S(2)}, u32[]{:S(2)}) %collective-permute-start.39) | collective-permute-done | bytes 786464 | tf_op jit(solution)/shard_map/ppermute | solution.py:20
  337.9 3.3 add_convert_fusion
  (146 shorter events, 67.1 us)
Async XLA Ops:
  0.0 20.8 %collective-permute-start.1 = (bf16[768,512]{1,0:T(8,128)(2,1)}, bf16[768,512]{1,0:T(8,128)(2,1)}, u32[]{:S(2)}, u32[]{:S(2)}) collective-permute-start(bf16[768,512]{1,0:T(8,128)(2,1)} %param.10), channel_id=1, source_target_pairs={{0,2},{1,3},{2,0},{3,1},{4,6},{5,7},{6,4},{7,5},{8,10},{9,11},{10,... | collective-permute-start | bytes 2359304 | tf_op jit(solution)/shard_map/ppermute | solution.py:20
  3.0 26.9 %collective-permute-start = (bf16[768,512]{1,0:T(8,128)(2,1)}, bf16[768,512]{1,0:T(8,128)(2,1)}, u32[]{:S(2)}, u32[]{:S(2)}) collective-permute-start(bf16[768,512]{1,0:T(8,128)(2,1)} %param.10), channel_id=1, source_target_pairs={{0,1},{1,0},{2,3},{3,2},{4,5},{5,4},{6,7},{7,6},{8,9},{9,8},{10,11... | collective-permute-start | bytes 2359304 | tf_op jit(solution)/shard_map/ppermute | solution.py:20
  20.9 43.8 %collective-permute-start.5 = (bf16[256,2048]{1,0:T(8,128)(2,1)S(1)}, bf16[256,2048]{1,0:T(8,128)(2,1)}, u32[]{:S(2)}, u32[]{:S(2)}) collective-permute-start(bf16[256,2048]{1,0:T(8,128)(2,1)S(1)} %pad_maximum_fusion.1), channel_id=1, source_target_pairs={{0,8},{4,12},{8,0},{12,4},{16,24},{20,28},{24,16},{28,20},{1,9},{5... | collective-permute-start | bytes 3145736 | tf_op jit(solution)/shard_map/ppermute | solution.py:20
  22.8 104.7 %collective-permute-start.14 = (bf16[256,2048]{1,0:T(8,128)(2,1)S(1)}, bf16[256,2048]{1,0:T(8,128)(2,1)}, u32[]{:S(2)}, u32[]{:S(2)}) collective-permute-start(bf16[256,2048]{1,0:T(8,128)(2,1)S(1)} %pad_maximum_fusion.1), channel_id=1, source_target_pairs={{0,4},{4,0},{8,12},{12,8},{16,20},{20,16},{24,28},{28,24},{1,5},{5... | collective-permute-start | bytes 3145736 | tf_op jit(solution)/shard_map/ppermute | solution.py:20
  28.2 154.4 %collective-permute-start.22 = (bf16[1024,256]{1,0:T(8,128)(2,1)}, bf16[1024,256]{1,0:T(8,128)(2,1)}, u32[]{:S(2)}, u32[]{:S(2)}) collective-permute-start(bf16[1024,256]{1,0:T(8,128)(2,1)} %get-tuple-element.27), channel_id=1, source_target_pairs={{0,8},{4,12},{8,0},{12,4},{16,24},{20,28},{24,16},{28,20},{1,9},{5... | collective-permute-start | bytes 1572872 | tf_op jit(solution)/shard_map/ppermute | solution.py:20
  29.8 90.0 %collective-permute-start.21 = (bf16[1024,256]{1,0:T(8,128)(2,1)}, bf16[1024,256]{1,0:T(8,128)(2,1)}, u32[]{:S(2)}, u32[]{:S(2)}) collective-permute-start(bf16[1024,256]{1,0:T(8,128)(2,1)} %get-tuple-element.27), channel_id=1, source_target_pairs={{0,4},{4,0},{8,12},{12,8},{16,20},{20,16},{24,28},{28,24},{1,5},{5... | collective-permute-start | bytes 1572872 | tf_op jit(solution)/shard_map/ppermute | solution.py:20
  39.7 22.4 %collective-permute-start.4 = (bf16[4,128,128]{2,1,0:T(8,128)(2,1)}, bf16[4,128,128]{2,1,0:T(8,128)(2,1)S(1)}, u32[]{:S(2)}, u32[]{:S(2)}) collective-permute-start(bf16[4,128,128]{2,1,0:T(8,128)(2,1)} %get-tuple-element.33), channel_id=1, source_target_pairs={{0,4},{4,0},{8,12},{12,8},{16,20},{20,16},{24,28},{28,24},{1,5},{5... | collective-permute-start | bytes 393224 | tf_op jit(solution)/shard_map/ppermute | solution.py:20
  62.1 54.7 %collective-permute-start.3 = (bf16[256,2048]{1,0:T(8,128)(2,1)}, bf16[256,2048]{1,0:T(8,128)(2,1)}, u32[]{:S(2)}, u32[]{:S(2)}) collective-permute-start(bf16[256,2048]{1,0:T(8,128)(2,1)} %pad_maximum_fusion), channel_id=1, source_target_pairs={{0,16},{4,20},{8,24},{12,28},{16,0},{20,4},{24,8},{28,12},{1,17},{... | collective-permute-start | bytes 3145736 | tf_op jit(solution)/shard_map/ppermute | solution.py:20
  64.8 25.0 %collective-permute-start.6 = (bf16[4,128,128]{2,1,0:T(8,128)(2,1)S(1)}, bf16[4,128,128]{2,1,0:T(8,128)(2,1)S(1)}, u32[]{:S(2)}, u32[]{:S(2)}) collective-permute-start(bf16[4,128,128]{2,1,0:T(8,128)(2,1)S(1)} %convert_element_type.122), channel_id=1, source_target_pairs={{0,8},{4,12},{8,0},{12,4},{16,24},{20,28},{24,16},{28,20},{1,9},{5... | collective-permute-start | bytes 393224 | tf_op jit(solution)/shard_map/ppermute | solution.py:20
  89.8 26.0 %collective-permute-start.7 = (bf16[4,128,128]{2,1,0:T(8,128)(2,1)S(1)}, bf16[4,128,128]{2,1,0:T(8,128)(2,1)}, u32[]{:S(2)}, u32[]{:S(2)}) collective-permute-start(bf16[4,128,128]{2,1,0:T(8,128)(2,1)S(1)} %fusion.39), channel_id=1, source_target_pairs={{0,16},{4,20},{8,24},{12,28},{16,0},{20,4},{24,8},{28,12},{1,17},{... | collective-permute-start | bytes 393224 | tf_op jit(solution)/shard_map/ppermute | solution.py:20
  121.8 31.3 %collective-permute-start.15 = (bf16[256,2048]{1,0:T(8,128)(2,1)}, bf16[256,2048]{1,0:T(8,128)(2,1)S(1)}, u32[]{:S(2)}, u32[]{:S(2)}) collective-permute-start(bf16[256,2048]{1,0:T(8,128)(2,1)} %collective-permute-done.5), channel_id=1, source_target_pairs={{0,4},{4,0},{8,12},{12,8},{16,20},{20,16},{24,28},{28,24},{1,5},{5... | collective-permute-start | bytes 3145736 | tf_op jit(solution)/shard_map/ppermute | solution.py:20
  126.6 28.6 %collective-permute-start.8 = (bf16[768,512]{1,0:T(8,128)(2,1)S(1)}, bf16[768,512]{1,0:T(8,128)(2,1)S(1)}, u32[]{:S(2)}, u32[]{:S(2)}) collective-permute-start(bf16[768,512]{1,0:T(8,128)(2,1)S(1)} %convolution_convert_fusion.8), channel_id=1, source_target_pairs={{0,1},{1,0},{2,3},{3,2},{4,5},{5,4},{6,7},{7,6},{8,9},{9,8},{10,11... | collective-permute-start | bytes 2359304 | tf_op jit(solution)/shard_map/ppermute | solution.py:20
  126.9 26.2 %collective-permute-start.24 = (bf16[1024,256]{1,0:T(8,128)(2,1)S(1)}, bf16[1024,256]{1,0:T(8,128)(2,1)S(1)}, u32[]{:S(2)}, u32[]{:S(2)}) collective-permute-start(bf16[1024,256]{1,0:T(8,128)(2,1)S(1)} %copy-done.10), channel_id=1, source_target_pairs={{0,16},{4,20},{8,24},{12,28},{16,0},{20,4},{24,8},{28,12},{1,17},{... | collective-permute-start | bytes 1572872 | tf_op jit(solution)/shard_map/ppermute | solution.py:20
  127.5 29.8 %collective-permute-start.10 = (bf16[768,512]{1,0:T(8,128)(2,1)S(1)}, bf16[768,512]{1,0:T(8,128)(2,1)S(1)}, u32[]{:S(2)}, u32[]{:S(2)}) collective-permute-start(bf16[768,512]{1,0:T(8,128)(2,1)S(1)} %add_convert_fusion.4), channel_id=1, source_target_pairs={{0,2},{1,3},{2,0},{3,1},{4,6},{5,7},{6,4},{7,5},{8,10},{9,11},{10,... | collective-permute-start | bytes 2359304 | tf_op jit(solution)/shard_map/ppermute | solution.py:20
  153.1 26.2 %collective-permute-start.16 = (bf16[256,2048]{1,0:T(8,128)(2,1)}, bf16[256,2048]{1,0:T(8,128)(2,1)S(1)}, u32[]{:S(2)}, u32[]{:S(2)}) collective-permute-start(bf16[256,2048]{1,0:T(8,128)(2,1)} %collective-permute-done.3), channel_id=1, source_target_pairs={{0,8},{4,12},{8,0},{12,4},{16,24},{20,28},{24,16},{28,20},{1,9},{5... | collective-permute-start | bytes 3145736 | tf_op jit(solution)/shard_map/ppermute | solution.py:20
  153.1 27.9 %collective-permute-start.17 = (bf16[256,2048]{1,0:T(8,128)(2,1)}, bf16[256,2048]{1,0:T(8,128)(2,1)S(1)}, u32[]{:S(2)}, u32[]{:S(2)}) collective-permute-start(bf16[256,2048]{1,0:T(8,128)(2,1)} %collective-permute-done.3), channel_id=1, source_target_pairs={{0,4},{4,0},{8,12},{12,8},{16,20},{20,16},{24,28},{28,24},{1,5},{5... | collective-permute-start | bytes 3145736 | tf_op jit(solution)/shard_map/ppermute | solution.py:20
  155.2 37.9 %collective-permute-start.25 = (bf16[1024,256]{1,0:T(8,128)(2,1)S(1)}, bf16[1024,256]{1,0:T(8,128)(2,1)S(1)}, u32[]{:S(2)}, u32[]{:S(2)}) collective-permute-start(bf16[1024,256]{1,0:T(8,128)(2,1)S(1)} %collective-permute-done.24), channel_id=1, source_target_pairs={{0,8},{4,12},{8,0},{12,4},{16,24},{20,28},{24,16},{28,20},{1,9},{5... | collective-permute-start | bytes 1572872 | tf_op jit(solution)/shard_map/ppermute | solution.py:20
  157.3 38.4 %collective-permute-start.26 = (bf16[1024,256]{1,0:T(8,128)(2,1)S(1)}, bf16[1024,256]{1,0:T(8,128)(2,1)S(1)}, u32[]{:S(2)}, u32[]{:S(2)}) collective-permute-start(bf16[1024,256]{1,0:T(8,128)(2,1)S(1)} %collective-permute-done.24), channel_id=1, source_target_pairs={{0,4},{4,0},{8,12},{12,8},{16,20},{20,16},{24,28},{28,24},{1,5},{5... | collective-permute-start | bytes 1572872 | tf_op jit(solution)/shard_map/ppermute | solution.py:20
  180.5 59.0 %collective-permute-start.18 = (bf16[256,2048]{1,0:T(8,128)(2,1)S(1)}, bf16[256,2048]{1,0:T(8,128)(2,1)S(1)}, u32[]{:S(2)}, u32[]{:S(2)}) collective-permute-start(bf16[256,2048]{1,0:T(8,128)(2,1)S(1)} %collective-permute-done.16), channel_id=1, source_target_pairs={{0,4},{4,0},{8,12},{12,8},{16,20},{20,16},{24,28},{28,24},{1,5},{5... | collective-permute-start | bytes 3145736 | tf_op jit(solution)/shard_map/ppermute | solution.py:20
  182.6 44.3 %collective-permute-start.31 = (bf16[768,512]{1,0:T(8,128)(2,1)S(1)}, bf16[768,512]{1,0:T(8,128)(2,1)S(1)}, u32[]{:S(2)}, u32[]{:S(2)}) collective-permute-start(bf16[768,512]{1,0:T(8,128)(2,1)S(1)} %get-tuple-element.24), channel_id=1, source_target_pairs={{0,16},{4,20},{8,24},{12,28},{16,0},{20,4},{24,8},{28,12},{1,17},{... | collective-permute-start | bytes 2359304 | tf_op jit(solution)/shard_map/ppermute | solution.py:20
  184.6 39.6 %collective-permute-start.23 = (bf16[1024,256]{1,0:T(8,128)(2,1)}, bf16[1024,256]{1,0:T(8,128)(2,1)S(1)}, u32[]{:S(2)}, u32[]{:S(2)}) collective-permute-start(bf16[1024,256]{1,0:T(8,128)(2,1)} %collective-permute-done.22), channel_id=1, source_target_pairs={{0,4},{4,0},{8,12},{12,8},{16,20},{20,16},{24,28},{28,24},{1,5},{5... | collective-permute-start | bytes 1572872 | tf_op jit(solution)/shard_map/ppermute | solution.py:20
  193.0 26.7 %collective-permute-start.35 = (f32[768]{0:T(1024)S(1)}, f32[768]{0:T(1024)S(1)}, u32[]{:S(2)}, u32[]{:S(2)}) collective-permute-start(f32[768]{0:T(1024)S(1)} %get-tuple-element.22), channel_id=1, source_target_pairs={{0,16},{4,20},{8,24},{12,28},{16,0},{20,4},{24,8},{28,12},{1,17},{... | collective-permute-start | bytes 9224 | tf_op jit(solution)/shard_map/ppermute | solution.py:20
  195.7 38.9 %collective-permute-start.27 = (bf16[1024,256]{1,0:T(8,128)(2,1)S(1)}, bf16[1024,256]{1,0:T(8,128)(2,1)S(1)}, u32[]{:S(2)}, u32[]{:S(2)}) collective-permute-start(bf16[1024,256]{1,0:T(8,128)(2,1)S(1)} %collective-permute-done.25), channel_id=1, source_target_pairs={{0,4},{4,0},{8,12},{12,8},{16,20},{20,16},{24,28},{28,24},{1,5},{5... | collective-permute-start | bytes 1572872 | tf_op jit(solution)/shard_map/ppermute | solution.py:20
  219.7 19.8 %collective-permute-start.12 = (bf16[768,512]{1,0:T(8,128)(2,1)S(1)}, bf16[768,512]{1,0:T(8,128)(2,1)S(1)}, u32[]{:S(2)}, u32[]{:S(2)}) collective-permute-start(bf16[768,512]{1,0:T(8,128)(2,1)S(1)} %get-tuple-element.24), channel_id=1, source_target_pairs={{0,2},{1,3},{2,0},{3,1},{4,6},{5,7},{6,4},{7,5},{8,10},{9,11},{10,... | collective-permute-start | bytes 2359304 | tf_op jit(solution)/shard_map/ppermute | solution.py:20
  224.3 15.3 %collective-permute-start.11 = (bf16[768,512]{1,0:T(8,128)(2,1)S(1)}, bf16[768,512]{1,0:T(8,128)(2,1)S(1)}, u32[]{:S(2)}, u32[]{:S(2)}) collective-permute-start(bf16[768,512]{1,0:T(8,128)(2,1)S(1)} %get-tuple-element.24), channel_id=1, source_target_pairs={{0,1},{1,0},{2,3},{3,2},{4,5},{5,4},{6,7},{7,6},{8,9},{9,8},{10,11... | collective-permute-start | bytes 2359304 | tf_op jit(solution)/shard_map/ppermute | solution.py:20
  226.9 27.9 %collective-permute-start.32 = (bf16[768,512]{1,0:T(8,128)(2,1)S(1)}, bf16[768,512]{1,0:T(8,128)(2,1)S(1)}, u32[]{:S(2)}, u32[]{:S(2)}) collective-permute-start(bf16[768,512]{1,0:T(8,128)(2,1)S(1)} %collective-permute-done.31), channel_id=1, source_target_pairs={{0,1},{1,0},{2,3},{3,2},{4,5},{5,4},{6,7},{7,6},{8,9},{9,8},{10,11... | collective-permute-start | bytes 2359304 | tf_op jit(solution)/shard_map/ppermute | solution.py:20
  234.6 20.2 %collective-permute-start.33 = (bf16[768,512]{1,0:T(8,128)(2,1)S(1)}, bf16[768,512]{1,0:T(8,128)(2,1)S(1)}, u32[]{:S(2)}, u32[]{:S(2)}) collective-permute-start(bf16[768,512]{1,0:T(8,128)(2,1)S(1)} %collective-permute-done.31), channel_id=1, source_target_pairs={{0,2},{1,3},{2,0},{3,1},{4,6},{5,7},{6,4},{7,5},{8,10},{9,11},{10,... | collective-permute-start | bytes 2359304 | tf_op jit(solution)/shard_map/ppermute | solution.py:20
  239.5 15.5 %collective-permute-start.13 = (bf16[768,512]{1,0:T(8,128)(2,1)S(1)}, bf16[768,512]{1,0:T(8,128)(2,1)S(1)}, u32[]{:S(2)}, u32[]{:S(2)}) collective-permute-start(bf16[768,512]{1,0:T(8,128)(2,1)S(1)} %collective-permute-done.12), channel_id=1, source_target_pairs={{0,1},{1,0},{2,3},{3,2},{4,5},{5,4},{6,7},{7,6},{8,9},{9,8},{10,11... | collective-permute-start | bytes 2359304 | tf_op jit(solution)/shard_map/ppermute | solution.py:20
  280.2 20.5 %collective-permute-start.38 = (bf16[768,512]{1,0:T(8,128)(2,1)S(1)}, bf16[768,512]{1,0:T(8,128)(2,1)S(1)}, u32[]{:S(2)}, u32[]{:S(2)}) collective-permute-start(bf16[768,512]{1,0:T(8,128)(2,1)S(1)} %add_convert_fusion.2), channel_id=1, source_target_pairs={{0,2},{1,3},{2,0},{3,1},{4,6},{5,7},{6,4},{7,5},{8,10},{9,11},{10,... | collective-permute-start | bytes 2359304 | tf_op jit(solution)/shard_map/ppermute | solution.py:20
  283.0 20.2 %collective-permute-start.28 = (bf16[768,512]{1,0:T(8,128)(2,1)S(1)}, bf16[768,512]{1,0:T(8,128)(2,1)S(1)}, u32[]{:S(2)}, u32[]{:S(2)}) collective-permute-start(bf16[768,512]{1,0:T(8,128)(2,1)S(1)} %convolution_convert_fusion.6), channel_id=1, source_target_pairs={{0,1},{1,0},{2,3},{3,2},{4,5},{5,4},{6,7},{7,6},{8,9},{9,8},{10,11... | collective-permute-start | bytes 2359304 | tf_op jit(solution)/shard_map/ppermute | solution.py:20
  285.3 31.2 %collective-permute-start.30 = (bf16[768,512]{1,0:T(8,128)(2,1)S(1)}, bf16[768,512]{1,0:T(8,128)(2,1)S(1)}, u32[]{:S(2)}, u32[]{:S(2)}) collective-permute-start(bf16[768,512]{1,0:T(8,128)(2,1)S(1)} %add_convert_fusion.3), channel_id=1, source_target_pairs={{0,2},{1,3},{2,0},{3,1},{4,6},{5,7},{6,4},{7,5},{8,10},{9,11},{10,... | collective-permute-start | bytes 2359304 | tf_op jit(solution)/shard_map/ppermute | solution.py:20
  303.1 34.8 %collective-permute-start.39 = (bf16[768,512]{1,0:T(8,128)(2,1)S(1)}, bf16[768,512]{1,0:T(8,128)(2,1)S(1)}, u32[]{:S(2)}, u32[]{:S(2)}) collective-permute-start(bf16[768,512]{1,0:T(8,128)(2,1)S(1)} %add_convert_fusion.1), channel_id=1, source_target_pairs={{0,16},{4,20},{8,24},{12,28},{16,0},{20,4},{24,8},{28,12},{1,17},{... | collective-permute-start | bytes 2359304 | tf_op jit(solution)/shard_map/ppermute | solution.py:20
  (22 other events, 268.6 us)
where the time goes:
time: 342 us; the launch traced here: 341 us
  waiting for transfers between devices  222 us (65%)
  matrix products  54.3 us (16%)
  starting transfers between devices  31.1 us (9%)
  local copies, waits for them, and re-layouts  28.7 us (8%)
  other arithmetic  4.11 us (1%)
    ppermute x40, waiting for transfers between devices, swap(): return lax.ppermute(value, axis, [(i, i ^ bit) for i in range(size)])  222 us
    dot_general x19, matrix products, matmul(): return jnp.dot(a, b, preferred_element_type=F32)  45.3 us
    ppermute x40, starting transfers between devices, swap(): return lax.ppermute(value, axis, [(i, i ^ bit) for i in range(size)])  31.1 us
    dynamic_update_slice x16, local copies, waits for them, and re-layouts, assemble(): out = lax.dynamic_update_slice_in_dim(out, piece, (me_seq ^ r) * rows, dim)  14 us
  transfers between devices with their start and end apart: 40, of which 17 were waited for; matrix products, arithmetic and copies ran while one was open for 21% of the time, Pallas kernels for 0%

commit v1 on v0

--- a/solution.py
+++ b/solution.py
@@ -22,7 +22,8 @@
     def spread(held, axis, bits):
         held = dict(held)
         for bit in bits:
-            held.update({r ^ bit: swap(v, axis, bit) for r, v in held.items()})
+            for r in list(held):
+                held[r ^ bit] = swap(held[r], axis, bit)
         return held
 
     def gather_tp(value):
@@ -91,7 +92,8 @@
         wide_give = jnp.concatenate([gate_give, up_give], axis=1)
         tall_own = {0: down_keep}
 
-        features = with_layout_constraint(side_by_side(gather_tp(tokens)), Layout((0, 1)))
+        token_pieces = gather_tp(tokens)
+        features = with_layout_constraint(side_by_side(token_pieces), Layout((0, 1)))
         wide_got = {pair: swap(wide_give, "seq", pair)}
         wide_far = dict(wide_own)
         for bit in first:
@@ -121,16 +123,18 @@
         (tall_give, history) = after({pair: down_give}, history)
         wide_got, history = after(wide_got, history)
         tall_got = {pair: swap(tall_give[pair], "seq", pair)}
+        got_near = hops({pair: wide_got[pair]}, last)
         for bit in first:
             wide_got.update(hops(wide_got, [bit]))
-        near = {**wide_near, **hops({r: v for r, v in wide_far.items() if r}, last)}
+        far_near = hops({r: v for r, v in wide_far.items() if r}, last)
+        near = {**wide_near, **far_near, **got_near}
         wide = {**wide_far, **near}
         scores = jnp.einsum("ihd,jhd->hij", query, keys, preferred_element_type=F32)
         causal = jnp.arange(length)[:, None] >= jnp.arange(length)[None, :]
         scores = jnp.where(causal[None], scores, 0.0).astype(BF16)
         inside = jnp.einsum("hij,jhd->ihd", scores, values, preferred_element_type=F32)
-        wide_got.update(hops(wide_got, last))
         wide.update(wide_got)
+        wide.update(hops({r: v for r, v in wide_got.items() if r != pair}, last))
         carried = jnp.einsum(
             "ihd,hde->ihe", query, history, preferred_element_type=F32
         )
@@ -138,7 +142,8 @@
         scale = lax.rsqrt(jnp.mean(mixed * mixed, axis=-1, keepdims=True) + 1e-06)
         normed = (mixed * scale * head_gain.reshape(heads, HD)).astype(BF16)
         normed = normed.reshape(length, heads * HD)
-        resid = tokens.astype(F32) + to_features(normed, w_out)
+        attended = to_features(normed, w_out)
+        resid = tokens.astype(F32) + attended
         gain = lax.dynamic_slice_in_dim(norm_gain, me_tp * width, width, 0)
         own_in = (resid * gain).astype(BF16)
         pair_in = swap(own_in, "seq", pair)
@@ -162,8 +167,9 @@
         def feed(pieces, total):
             factor = lax.rsqrt(total / model + 1e-05)[:, None]
             ffn_in = side_by_side(pieces)
-            gate = matmul(ffn_in, gate_whole) * factor
+            gate = matmul(ffn_in, gate_whole)
             upward = matmul(ffn_in, up_whole) * factor
+            gate = gate * factor
             hidden = (jax.nn.silu(gate) * upward).astype(BF16)
             return to_features(hidden, down_whole)
 

time: 342 us -> 314 us (0.918)
  waiting for transfers between devices: 222 us -> 192 us
  starting transfers between devices: 31.1 us -> 35.6 us
    ppermute x40, waiting for transfers between devices: 222 us -> 192 us  [swap(): return lax.ppermute(value, axis, [(i, i ^ bit) for i in range(size)])]
    ppermute x40, starting transfers between devices: 31.1 us -> 35.6 us  [swap(): return lax.ppermute(value, axis, [(i, i ^ bit) for i in range(size)])]
  transfers between devices with their start and end apart: 40 -> 40, of which waited for: 17 -> 17; matrix products, arithmetic and copies ran while one was open for 21% -> 22% of each run, Pallas kernels for 0% -> 0%
where the time goes in v1:
time: 314 us; the launch traced here: 313 us
  waiting for transfers between devices  192 us (61%)
  matrix products  54.2 us (17%)
  starting transfers between devices  35.6 us (11%)
  local copies, waits for them, and re-layouts  26.5 us (8%)
  other arithmetic  4.11 us (1%)
    ppermute x40, waiting for transfers between devices, swap(): return lax.ppermute(value, axis, [(i, i ^ bit) for i in range(size)])  192 us
    dot_general x19, matrix products, matmul(): return jnp.dot(a, b, preferred_element_type=F32)  45.2 us
    ppermute x40, starting transfers between devices, swap(): return lax.ppermute(value, axis, [(i, i ^ bit) for i in range(size)])  35.6 us
    dynamic_update_slice x16, local copies, waits for them, and re-layouts, assemble(): out = lax.dynamic_update_slice_in_dim(out, piece, (me_seq ^ r) * rows, dim)  12.9 us
  transfers between devices with their start and end apart: 40, of which 17 were waited for; matrix products, arithmetic and copies ran while one was open for 22% of the time, Pallas kernels for 0%

profile of v1, /device:TPU:0, one launch (start us, length us, event | category | flops | bytes accessed | tf_op | source)
XLA Modules:
  0.0 313.2 jit_solution(14809092255741234243)
XLA Ops:
  0.0 3.0 collective-permute-start.1
  4.7 16.1 %collective-permute-done.1 = bf16[768,512]{1,0:T(8,128)(2,1)} collective-permute-done((bf16[768,512]{1,0:T(8,128)(2,1)}, bf16[768,512]{1,0:T(8,128)(2,1)}, u32[]{:S(2)}, u32[]{:S(2)}) %collective-permute-start.1) | collective-permute-done | bytes 786464 | tf_op jit(solution)/shard_map/ppermute | solution.py:20
  25.4 2.6 collective-permute-start.3
  39.3 2.5 broadcast_in_dim.35
  46.3 5.3 %collective-permute-done.4 = bf16[4,128,128]{2,1,0:T(8,128)(2,1)S(1)} collective-permute-done((bf16[4,128,128]{2,1,0:T(8,128)(2,1)}, bf16[4,128,128]{2,1,0:T(8,128)(2,1)S(1)}, u32[]{:S(2)}, u32[]{:S(2)}) %collective-permute-start.4) | collective-permute-done | bytes 131104 | tf_op jit(solution)/shard_map/ppermute | solution.py:20
  51.7 14.9 %collective-permute-done.5 = bf16[256,2048]{1,0:T(8,128)(2,1)} collective-permute-done((bf16[256,2048]{1,0:T(8,128)(2,1)S(1)}, bf16[256,2048]{1,0:T(8,128)(2,1)}, u32[]{:S(2)}, u32[]{:S(2)}) %collective-permute-start.5) | collective-permute-done | bytes 1048608 | tf_op jit(solution)/shard_map/ppermute | solution.py:20
  66.7 5.3 %convolution_convert_fusion.1 = bf16[768,512]{0,1:T(8,128)(2,1)} fusion(bf16[768,2048]{1,0:T(8,128)(2,1)} %copy-done.2, bf16[2048,512]{1,0:T(8,128)(2,1)} %param.11), kind=kOutput, calls=%fused_computation.31 | convolution fusion | flops 1611005952 | bytes 6029312 | tf_op jit(solution)/shard_map/dot_general | solution.py:72
  72.0 2.4 collective-permute-done.6
  76.3 5.9 %fusion = f32[4,128,768]{2,1,0:T(8,128)} fusion(bf16[768,4,128]{0,2,1:T(8,128)(2,1)} %bitcast.50, pred[768,768]{1,0:T(8,128)(4,1)} %iota_compare_fusion, bf16[768,4,128]{0,2,1:T(8,128)(2,1)} %bitcast.47, bf16[768,4,128]{0,2,1:T(8,128)(2,1)} %bitcast.52), kind=kOutput, calls=%fused_computation.1 | convolution fusion | flops 1212678144 | bytes 4521984 | tf_op jit(solution)/shard_map/hij,jhd->ihd/dot_general | solution.py:135
  99.1 21.3 %collective-permute-done.24 = bf16[1024,256]{1,0:T(8,128)(2,1)S(1)} collective-permute-done((bf16[1024,256]{1,0:T(8,128)(2,1)S(1)}, bf16[1024,256]{1,0:T(8,128)(2,1)S(1)}, u32[]{:S(2)}, u32[]{:S(2)}) %collective-permute-start.24) | collective-permute-done | bytes 524320 | tf_op jit(solution)/shard_map/ppermute | solution.py:20
  122.6 14.4 %collective-permute-done.16 = bf16[256,2048]{1,0:T(8,128)(2,1)S(1)} collective-permute-done((bf16[256,2048]{1,0:T(8,128)(2,1)}, bf16[256,2048]{1,0:T(8,128)(2,1)S(1)}, u32[]{:S(2)}, u32[]{:S(2)}) %collective-permute-start.16) | collective-permute-done | bytes 1048608 | tf_op jit(solution)/shard_map/ppermute | solution.py:20
  143.0 14.9 %collective-permute-done.17 = bf16[256,2048]{1,0:T(8,128)(2,1)S(1)} collective-permute-done((bf16[256,2048]{1,0:T(8,128)(2,1)}, bf16[256,2048]{1,0:T(8,128)(2,1)S(1)}, u32[]{:S(2)}, u32[]{:S(2)}) %collective-permute-start.17) | collective-permute-done | bytes 1048608 | tf_op jit(solution)/shard_map/ppermute | solution.py:20
  163.6 11.1 %collective-permute-done.25 = bf16[1024,256]{1,0:T(8,128)(2,1)S(1)} collective-permute-done((bf16[1024,256]{1,0:T(8,128)(2,1)S(1)}, bf16[1024,256]{1,0:T(8,128)(2,1)S(1)}, u32[]{:S(2)}, u32[]{:S(2)}) %collective-permute-start.25) | collective-permute-done | bytes 524320 | tf_op jit(solution)/shard_map/ppermute | solution.py:20
  175.5 2.7 collective-permute-start.27
  178.2 16.4 %collective-permute-done.35 = f32[768]{0:T(1024)S(1)} collective-permute-done((f32[768]{0:T(1024)S(1)}, f32[768]{0:T(1024)S(1)}, u32[]{:S(2)}, u32[]{:S(2)}) %collective-permute-start.35) | collective-permute-done | bytes 3104 | tf_op jit(solution)/shard_map/ppermute | solution.py:20
  198.3 3.8 %collective-permute-done.27 = bf16[1024,256]{1,0:T(8,128)(2,1)S(1)} collective-permute-done((bf16[1024,256]{1,0:T(8,128)(2,1)S(1)}, bf16[1024,256]{1,0:T(8,128)(2,1)S(1)}, u32[]{:S(2)}, u32[]{:S(2)}) %collective-permute-start.27) | collective-permute-done | bytes 524320 | tf_op jit(solution)/shard_map/ppermute | solution.py:20
  205.3 9.7 %collective-permute-done.12 = bf16[768,512]{1,0:T(8,128)(2,1)S(1)} collective-permute-done((bf16[768,512]{1,0:T(8,128)(2,1)S(1)}, bf16[768,512]{1,0:T(8,128)(2,1)S(1)}, u32[]{:S(2)}, u32[]{:S(2)}) %collective-permute-start.12) | collective-permute-done | bytes 786464 | tf_op jit(solution)/shard_map/ppermute | solution.py:20
  215.9 10.2 %collective-permute-done.33 = bf16[768,512]{1,0:T(8,128)(2,1)S(1)} collective-permute-done((bf16[768,512]{1,0:T(8,128)(2,1)S(1)}, bf16[768,512]{1,0:T(8,128)(2,1)S(1)}, u32[]{:S(2)}, u32[]{:S(2)}) %collective-permute-start.33) | collective-permute-done | bytes 786464 | tf_op jit(solution)/shard_map/ppermute | solution.py:20
  226.4 3.4 %fusion.11 = f32[768,1024]{1,0:T(8,128)S(1)} fusion(bf16[768,2048]{1,0:T(8,128)(2,1)S(1)} %constant_dynamic-update-slice_fusion.20, bf16[2048,2048]{1,0:T(8,128)(2,1)S(1)} %constant_dynamic-update-slice_fusion.12), kind=kOutput, calls=%fused_computation.11 | convolution fusion | flops 3221225472 | bytes 10485760 | tf_op jit(solution)/shard_map/dot_general | solution.py:72
  230.0 3.4 %fusion.9 = f32[768,1024]{1,0:T(8,128)S(1)} fusion(bf16[768,2048]{1,0:T(8,128)(2,1)S(1)} %constant_dynamic-update-slice_fusion, bf16[2048,2048]{1,0:T(8,128)(2,1)S(1)} %constant_dynamic-update-slice_fusion.12), kind=kOutput, calls=%fused_computation.9 | convolution fusion | flops 3221225472 | bytes 10485760 | tf_op jit(solution)/shard_map/dot_general | solution.py:72
  233.4 4.1 %multiply_convert_fusion = bf16[768,1024]{1,0:T(8,128)(2,1)S(1)} fusion(f32[768,1024]{1,0:T(8,128)S(1)} %fusion.9, bf16[768,2048]{1,0:T(8,128)(2,1)S(1)} %constant_dynamic-update-slice_fusion, bf16[2048,2048]{1,0:T(8,128)(2,1)S(1)} %constant_dynamic-update-slice_fusion.12, f32[768]{0:T(1024)S(1)} %add_rsqrt_fusion.1), kind=kOutput, calls=%fused_computation.13 | convolution fusion | flops 3227516928 | bytes 12062720 | tf_op jit(solution)/shard_map/dot_general | solution.py:72
  237.5 2.2 convolution_convert_fusion.3
  240.3 3.8 %multiply_convert_fusion.1 = bf16[768,1024]{1,0:T(8,128)(2,1)S(1)} fusion(f32[768,1024]{1,0:T(8,128)S(1)} %fusion.11, bf16[768,2048]{1,0:T(8,128)(2,1)S(1)} %constant_dynamic-update-slice_fusion.20, bf16[2048,2048]{1,0:T(8,128)(2,1)S(1)} %constant_dynamic-update-slice_fusion.12, f32[768]{0:T(1024)S(1)} %get-tuple-element.21), kind=kOutput, calls=%fused_computation.14 | convolution fusion | flops 3227516928 | bytes 12062720 | tf_op jit(solution)/shard_map/dot_general | solution.py:72
  244.1 2.2 convolution_convert_fusion.5
  246.4 2.2 convolution_convert_fusion.4
  249.2 2.2 add_convert_fusion.2
  254.3 2.2 add_convert_fusion.3
  258.1 13.8 %collective-permute-done.38 = bf16[768,512]{1,0:T(8,128)(2,1)S(1)} collective-permute-done((bf16[768,512]{1,0:T(8,128)(2,1)S(1)}, bf16[768,512]{1,0:T(8,128)(2,1)S(1)}, u32[]{:S(2)}, u32[]{:S(2)}) %collective-permute-start.38) | collective-permute-done | bytes 786464 | tf_op jit(solution)/shard_map/ppermute | solution.py:20
  271.9 2.4 add_convert_fusion.1
  274.4 13.4 %collective-permute-done.30 = bf16[768,512]{1,0:T(8,128)(2,1)S(1)} collective-permute-done((bf16[768,512]{1,0:T(8,128)(2,1)S(1)}, bf16[768,512]{1,0:T(8,128)(2,1)S(1)}, u32[]{:S(2)}, u32[]{:S(2)}) %collective-permute-start.30) | collective-permute-done | bytes 786464 | tf_op jit(solution)/shard_map/ppermute | solution.py:20
  287.8 22.0 %collective-permute-done.39 = bf16[768,512]{1,0:T(8,128)(2,1)S(1)} collective-permute-done((bf16[768,512]{1,0:T(8,128)(2,1)S(1)}, bf16[768,512]{1,0:T(8,128)(2,1)S(1)}, u32[]{:S(2)}, u32[]{:S(2)}) %collective-permute-start.39) | collective-permute-done | bytes 786464 | tf_op jit(solution)/shard_map/ppermute | solution.py:20
  309.8 3.3 %add_convert_fusion = bf16[768,512]{1,0:T(8,128)(2,1)} fusion(bf16[768,512]{1,0:T(8,128)(2,1)S(1)} %collective-permute-done.39, f32[768,512]{1,0:T(8,128)S(1)} %get-tuple-element.25, bf16[768,512]{1,0:T(8,128)(2,1)S(1)} %collective-permute-done.30, bf16[768,512]{1,0:T(8,128)(2,1)S(1)} %collective-permute-done.28, ...), kind=kOutput, calls=%fused_computation.21 | convolution fusion | flops 808452096 | bytes 7340036 | tf_op jit(solution)/shard_map/dot_general | solution.py:72
  (142 shorter events, 69.2 us)
Async XLA Ops:
  0.0 20.8 %collective-permute-start.1 = (bf16[768,512]{1,0:T(8,128)(2,1)}, bf16[768,512]{1,0:T(8,128)(2,1)}, u32[]{:S(2)}, u32[]{:S(2)}) collective-permute-start(bf16[768,512]{1,0:T(8,128)(2,1)} %param.10), channel_id=1, source_target_pairs={{0,2},{1,3},{2,0},{3,1},{4,6},{5,7},{6,4},{7,5},{8,10},{9,11},{10,... | collective-permute-start | bytes 2359304 | tf_op jit(solution)/shard_map/ppermute | solution.py:20
  3.0 26.2 %collective-permute-start = (bf16[768,512]{1,0:T(8,128)(2,1)}, bf16[768,512]{1,0:T(8,128)(2,1)}, u32[]{:S(2)}, u32[]{:S(2)}) collective-permute-start(bf16[768,512]{1,0:T(8,128)(2,1)} %param.10), channel_id=1, source_target_pairs={{0,1},{1,0},{2,3},{3,2},{4,5},{5,4},{6,7},{7,6},{8,9},{9,8},{10,11... | collective-permute-start | bytes 2359304 | tf_op jit(solution)/shard_map/ppermute | solution.py:20
  20.8 11.0 %collective-permute-start.2 = (bf16[768,512]{1,0:T(8,128)(2,1)}, bf16[768,512]{1,0:T(8,128)(2,1)}, u32[]{:S(2)}, u32[]{:S(2)}) collective-permute-start(bf16[768,512]{1,0:T(8,128)(2,1)} %collective-permute-done.1), channel_id=1, source_target_pairs={{0,1},{1,0},{2,3},{3,2},{4,5},{5,4},{6,7},{7,6},{8,9},{9,8},{10,11... | collective-permute-start | bytes 2359304 | tf_op jit(solution)/shard_map/ppermute | solution.py:20
  20.9 45.7 %collective-permute-start.5 = (bf16[256,2048]{1,0:T(8,128)(2,1)S(1)}, bf16[256,2048]{1,0:T(8,128)(2,1)}, u32[]{:S(2)}, u32[]{:S(2)}) collective-permute-start(bf16[256,2048]{1,0:T(8,128)(2,1)S(1)} %pad_maximum_fusion.1), channel_id=1, source_target_pairs={{0,8},{4,12},{8,0},{12,4},{16,24},{20,28},{24,16},{28,20},{1,9},{5... | collective-permute-start | bytes 3145736 | tf_op jit(solution)/shard_map/ppermute | solution.py:20
  22.8 72.8 %collective-permute-start.14 = (bf16[256,2048]{1,0:T(8,128)(2,1)S(1)}, bf16[256,2048]{1,0:T(8,128)(2,1)}, u32[]{:S(2)}, u32[]{:S(2)}) collective-permute-start(bf16[256,2048]{1,0:T(8,128)(2,1)S(1)} %pad_maximum_fusion.1), channel_id=1, source_target_pairs={{0,4},{4,0},{8,12},{12,8},{16,20},{20,16},{24,28},{28,24},{1,5},{5... | collective-permute-start | bytes 3145736 | tf_op jit(solution)/shard_map/ppermute | solution.py:20
  25.4 58.1 %collective-permute-start.3 = (bf16[256,2048]{1,0:T(8,128)(2,1)}, bf16[256,2048]{1,0:T(8,128)(2,1)}, u32[]{:S(2)}, u32[]{:S(2)}) collective-permute-start(bf16[256,2048]{1,0:T(8,128)(2,1)} %pad_maximum_fusion), channel_id=1, source_target_pairs={{0,16},{4,20},{8,24},{12,28},{16,0},{20,4},{24,8},{28,12},{1,17},{... | collective-permute-start | bytes 3145736 | tf_op jit(solution)/shard_map/ppermute | solution.py:20
  38.8 12.9 %collective-permute-start.4 = (bf16[4,128,128]{2,1,0:T(8,128)(2,1)}, bf16[4,128,128]{2,1,0:T(8,128)(2,1)S(1)}, u32[]{:S(2)}, u32[]{:S(2)}) collective-permute-start(bf16[4,128,128]{2,1,0:T(8,128)(2,1)} %get-tuple-element.33), channel_id=1, source_target_pairs={{0,4},{4,0},{8,12},{12,8},{16,20},{20,16},{24,28},{28,24},{1,5},{5... | collective-permute-start | bytes 393224 | tf_op jit(solution)/shard_map/ppermute | solution.py:20
  43.0 43.5 %collective-permute-start.21 = (bf16[1024,256]{1,0:T(8,128)(2,1)}, bf16[1024,256]{1,0:T(8,128)(2,1)}, u32[]{:S(2)}, u32[]{:S(2)}) collective-permute-start(bf16[1024,256]{1,0:T(8,128)(2,1)} %get-tuple-element.27), channel_id=1, source_target_pairs={{0,4},{4,0},{8,12},{12,8},{16,20},{20,16},{24,28},{28,24},{1,5},{5... | collective-permute-start | bytes 1572872 | tf_op jit(solution)/shard_map/ppermute | solution.py:20
  88.4 32.0 %collective-permute-start.15 = (bf16[256,2048]{1,0:T(8,128)(2,1)}, bf16[256,2048]{1,0:T(8,128)(2,1)S(1)}, u32[]{:S(2)}, u32[]{:S(2)}) collective-permute-start(bf16[256,2048]{1,0:T(8,128)(2,1)} %collective-permute-done.5), channel_id=1, source_target_pairs={{0,4},{4,0},{8,12},{12,8},{16,20},{20,16},{24,28},{28,24},{1,5},{5... | collective-permute-start | bytes 3145736 | tf_op jit(solution)/shard_map/ppermute | solution.py:20
  93.8 45.2 %collective-permute-start.8 = (bf16[768,512]{1,0:T(8,128)(2,1)S(1)}, bf16[768,512]{1,0:T(8,128)(2,1)S(1)}, u32[]{:S(2)}, u32[]{:S(2)}) collective-permute-start(bf16[768,512]{1,0:T(8,128)(2,1)S(1)} %convolution_convert_fusion.8), channel_id=1, source_target_pairs={{0,1},{1,0},{2,3},{3,2},{4,5},{5,4},{6,7},{7,6},{8,9},{9,8},{10,11... | collective-permute-start | bytes 2359304 | tf_op jit(solution)/shard_map/ppermute | solution.py:20
  94.1 42.9 %collective-permute-start.16 = (bf16[256,2048]{1,0:T(8,128)(2,1)}, bf16[256,2048]{1,0:T(8,128)(2,1)S(1)}, u32[]{:S(2)}, u32[]{:S(2)}) collective-permute-start(bf16[256,2048]{1,0:T(8,128)(2,1)} %collective-permute-done.3), channel_id=1, source_target_pairs={{0,4},{4,0},{8,12},{12,8},{16,20},{20,16},{24,28},{28,24},{1,5},{5... | collective-permute-start | bytes 3145736 | tf_op jit(solution)/shard_map/ppermute | solution.py:20
  94.4 26.1 %collective-permute-start.24 = (bf16[1024,256]{1,0:T(8,128)(2,1)S(1)}, bf16[1024,256]{1,0:T(8,128)(2,1)S(1)}, u32[]{:S(2)}, u32[]{:S(2)}) collective-permute-start(bf16[1024,256]{1,0:T(8,128)(2,1)S(1)} %copy-done.8), channel_id=1, source_target_pairs={{0,16},{4,20},{8,24},{12,28},{16,0},{20,4},{24,8},{28,12},{1,17},{... | collective-permute-start | bytes 1572872 | tf_op jit(solution)/shard_map/ppermute | solution.py:20
  95.6 44.9 %collective-permute-start.10 = (bf16[768,512]{1,0:T(8,128)(2,1)S(1)}, bf16[768,512]{1,0:T(8,128)(2,1)S(1)}, u32[]{:S(2)}, u32[]{:S(2)}) collective-permute-start(bf16[768,512]{1,0:T(8,128)(2,1)S(1)} %add_convert_fusion.4), channel_id=1, source_target_pairs={{0,2},{1,3},{2,0},{3,1},{4,6},{5,7},{6,4},{7,5},{8,10},{9,11},{10,... | collective-permute-start | bytes 2359304 | tf_op jit(solution)/shard_map/ppermute | solution.py:20
  120.4 40.7 %collective-permute-start.22 = (bf16[1024,256]{1,0:T(8,128)(2,1)}, bf16[1024,256]{1,0:T(8,128)(2,1)S(1)}, u32[]{:S(2)}, u32[]{:S(2)}) collective-permute-start(bf16[1024,256]{1,0:T(8,128)(2,1)} %get-tuple-element.27), channel_id=1, source_target_pairs={{0,8},{4,12},{8,0},{12,4},{16,24},{20,28},{24,16},{28,20},{1,9},{5... | collective-permute-start | bytes 1572872 | tf_op jit(solution)/shard_map/ppermute | solution.py:20
  120.4 37.5 %collective-permute-start.17 = (bf16[256,2048]{1,0:T(8,128)(2,1)}, bf16[256,2048]{1,0:T(8,128)(2,1)S(1)}, u32[]{:S(2)}, u32[]{:S(2)}) collective-permute-start(bf16[256,2048]{1,0:T(8,128)(2,1)} %collective-permute-done.3), channel_id=1, source_target_pairs={{0,8},{4,12},{8,0},{12,4},{16,24},{20,28},{24,16},{28,20},{1,9},{5... | collective-permute-start | bytes 3145736 | tf_op jit(solution)/shard_map/ppermute | solution.py:20
  137.0 37.7 %collective-permute-start.25 = (bf16[1024,256]{1,0:T(8,128)(2,1)S(1)}, bf16[1024,256]{1,0:T(8,128)(2,1)S(1)}, u32[]{:S(2)}, u32[]{:S(2)}) collective-permute-start(bf16[1024,256]{1,0:T(8,128)(2,1)S(1)} %collective-permute-done.24), channel_id=1, source_target_pairs={{0,8},{4,12},{8,0},{12,4},{16,24},{20,28},{24,16},{28,20},{1,9},{5... | collective-permute-start | bytes 1572872 | tf_op jit(solution)/shard_map/ppermute | solution.py:20
  139.0 36.5 %collective-permute-start.26 = (bf16[1024,256]{1,0:T(8,128)(2,1)S(1)}, bf16[1024,256]{1,0:T(8,128)(2,1)S(1)}, u32[]{:S(2)}, u32[]{:S(2)}) collective-permute-start(bf16[1024,256]{1,0:T(8,128)(2,1)S(1)} %collective-permute-done.24), channel_id=1, source_target_pairs={{0,4},{4,0},{8,12},{12,8},{16,20},{20,16},{24,28},{28,24},{1,5},{5... | collective-permute-start | bytes 1572872 | tf_op jit(solution)/shard_map/ppermute | solution.py:20
  141.6 18.0 %collective-permute-start.19 = (f32[768]{0:T(1024)S(1)}, f32[768]{0:T(1024)S(1)}, u32[]{:S(2)}, u32[]{:S(2)}) collective-permute-start(f32[768]{0:T(1024)S(1)} %multiply_reduce_fusion), channel_id=1, source_target_pairs={{0,1},{1,0},{2,3},{3,2},{4,5},{5,4},{6,7},{7,6},{8,9},{9,8},{10,11... | collective-permute-start | bytes 9224 | tf_op jit(solution)/shard_map/ppermute | solution.py:20
  157.9 57.1 %collective-permute-start.18 = (bf16[256,2048]{1,0:T(8,128)(2,1)S(1)}, bf16[256,2048]{1,0:T(8,128)(2,1)S(1)}, u32[]{:S(2)}, u32[]{:S(2)}) collective-permute-start(bf16[256,2048]{1,0:T(8,128)(2,1)S(1)} %collective-permute-done.17), channel_id=1, source_target_pairs={{0,4},{4,0},{8,12},{12,8},{16,20},{20,16},{24,28},{28,24},{1,5},{5... | collective-permute-start | bytes 3145736 | tf_op jit(solution)/shard_map/ppermute | solution.py:20
  161.2 36.6 %collective-permute-start.31 = (bf16[768,512]{1,0:T(8,128)(2,1)S(1)}, bf16[768,512]{1,0:T(8,128)(2,1)S(1)}, u32[]{:S(2)}, u32[]{:S(2)}) collective-permute-start(bf16[768,512]{1,0:T(8,128)(2,1)S(1)} %get-tuple-element.24), channel_id=1, source_target_pairs={{0,16},{4,20},{8,24},{12,28},{16,0},{20,4},{24,8},{28,12},{1,17},{... | collective-permute-start | bytes 2359304 | tf_op jit(solution)/shard_map/ppermute | solution.py:20
  163.2 32.0 %collective-permute-start.23 = (bf16[1024,256]{1,0:T(8,128)(2,1)S(1)}, bf16[1024,256]{1,0:T(8,128)(2,1)S(1)}, u32[]{:S(2)}, u32[]{:S(2)}) collective-permute-start(bf16[1024,256]{1,0:T(8,128)(2,1)S(1)} %collective-permute-done.22), channel_id=1, source_target_pairs={{0,4},{4,0},{8,12},{12,8},{16,20},{20,16},{24,28},{28,24},{1,5},{5... | collective-permute-start | bytes 1572872 | tf_op jit(solution)/shard_map/ppermute | solution.py:20
  174.7 20.0 %collective-permute-start.35 = (f32[768]{0:T(1024)S(1)}, f32[768]{0:T(1024)S(1)}, u32[]{:S(2)}, u32[]{:S(2)}) collective-permute-start(f32[768]{0:T(1024)S(1)} %get-tuple-element.22), channel_id=1, source_target_pairs={{0,16},{4,20},{8,24},{12,28},{16,0},{20,4},{24,8},{28,12},{1,17},{... | collective-permute-start | bytes 9224 | tf_op jit(solution)/shard_map/ppermute | solution.py:20
  175.5 26.6 %collective-permute-start.27 = (bf16[1024,256]{1,0:T(8,128)(2,1)S(1)}, bf16[1024,256]{1,0:T(8,128)(2,1)S(1)}, u32[]{:S(2)}, u32[]{:S(2)}) collective-permute-start(bf16[1024,256]{1,0:T(8,128)(2,1)S(1)} %collective-permute-done.25), channel_id=1, source_target_pairs={{0,4},{4,0},{8,12},{12,8},{16,20},{20,16},{24,28},{28,24},{1,5},{5... | collective-permute-start | bytes 1572872 | tf_op jit(solution)/shard_map/ppermute | solution.py:20
  194.6 20.4 %collective-permute-start.12 = (bf16[768,512]{1,0:T(8,128)(2,1)S(1)}, bf16[768,512]{1,0:T(8,128)(2,1)S(1)}, u32[]{:S(2)}, u32[]{:S(2)}) collective-permute-start(bf16[768,512]{1,0:T(8,128)(2,1)S(1)} %get-tuple-element.24), channel_id=1, source_target_pairs={{0,2},{1,3},{2,0},{3,1},{4,6},{5,7},{6,4},{7,5},{8,10},{9,11},{10,... | collective-permute-start | bytes 2359304 | tf_op jit(solution)/shard_map/ppermute | solution.py:20
  195.2 20.0 %collective-permute-start.11 = (bf16[768,512]{1,0:T(8,128)(2,1)S(1)}, bf16[768,512]{1,0:T(8,128)(2,1)S(1)}, u32[]{:S(2)}, u32[]{:S(2)}) collective-permute-start(bf16[768,512]{1,0:T(8,128)(2,1)S(1)} %get-tuple-element.24), channel_id=1, source_target_pairs={{0,1},{1,0},{2,3},{3,2},{4,5},{5,4},{6,7},{7,6},{8,9},{9,8},{10,11... | collective-permute-start | bytes 2359304 | tf_op jit(solution)/shard_map/ppermute | solution.py:20
  197.8 28.3 %collective-permute-start.32 = (bf16[768,512]{1,0:T(8,128)(2,1)S(1)}, bf16[768,512]{1,0:T(8,128)(2,1)S(1)}, u32[]{:S(2)}, u32[]{:S(2)}) collective-permute-start(bf16[768,512]{1,0:T(8,128)(2,1)S(1)} %collective-permute-done.31), channel_id=1, source_target_pairs={{0,1},{1,0},{2,3},{3,2},{4,5},{5,4},{6,7},{7,6},{8,9},{9,8},{10,11... | collective-permute-start | bytes 2359304 | tf_op jit(solution)/shard_map/ppermute | solution.py:20
  202.1 24.0 %collective-permute-start.33 = (bf16[768,512]{1,0:T(8,128)(2,1)S(1)}, bf16[768,512]{1,0:T(8,128)(2,1)S(1)}, u32[]{:S(2)}, u32[]{:S(2)}) collective-permute-start(bf16[768,512]{1,0:T(8,128)(2,1)S(1)} %collective-permute-done.31), channel_id=1, source_target_pairs={{0,2},{1,3},{2,0},{3,1},{4,6},{5,7},{6,4},{7,5},{8,10},{9,11},{10,... | collective-permute-start | bytes 2359304 | tf_op jit(solution)/shard_map/ppermute | solution.py:20
  215.0 11.3 %collective-permute-start.13 = (bf16[768,512]{1,0:T(8,128)(2,1)S(1)}, bf16[768,512]{1,0:T(8,128)(2,1)S(1)}, u32[]{:S(2)}, u32[]{:S(2)}) collective-permute-start(bf16[768,512]{1,0:T(8,128)(2,1)S(1)} %collective-permute-done.12), channel_id=1, source_target_pairs={{0,1},{1,0},{2,3},{3,2},{4,5},{5,4},{6,7},{7,6},{8,9},{9,8},{10,11... | collective-permute-start | bytes 2359304 | tf_op jit(solution)/shard_map/ppermute | solution.py:20
  251.4 20.5 %collective-permute-start.38 = (bf16[768,512]{1,0:T(8,128)(2,1)S(1)}, bf16[768,512]{1,0:T(8,128)(2,1)S(1)}, u32[]{:S(2)}, u32[]{:S(2)}) collective-permute-start(bf16[768,512]{1,0:T(8,128)(2,1)S(1)} %add_convert_fusion.2), channel_id=1, source_target_pairs={{0,2},{1,3},{2,0},{3,1},{4,6},{5,7},{6,4},{7,5},{8,10},{9,11},{10,... | collective-permute-start | bytes 2359304 | tf_op jit(solution)/shard_map/ppermute | solution.py:20
  254.2 20.2 %collective-permute-start.28 = (bf16[768,512]{1,0:T(8,128)(2,1)S(1)}, bf16[768,512]{1,0:T(8,128)(2,1)S(1)}, u32[]{:S(2)}, u32[]{:S(2)}) collective-permute-start(bf16[768,512]{1,0:T(8,128)(2,1)S(1)} %convolution_convert_fusion.6), channel_id=1, source_target_pairs={{0,1},{1,0},{2,3},{3,2},{4,5},{5,4},{6,7},{7,6},{8,9},{9,8},{10,11... | collective-permute-start | bytes 2359304 | tf_op jit(solution)/shard_map/ppermute | solution.py:20
  256.5 31.3 %collective-permute-start.30 = (bf16[768,512]{1,0:T(8,128)(2,1)S(1)}, bf16[768,512]{1,0:T(8,128)(2,1)S(1)}, u32[]{:S(2)}, u32[]{:S(2)}) collective-permute-start(bf16[768,512]{1,0:T(8,128)(2,1)S(1)} %add_convert_fusion.3), channel_id=1, source_target_pairs={{0,2},{1,3},{2,0},{3,1},{4,6},{5,7},{6,4},{7,5},{8,10},{9,11},{10,... | collective-permute-start | bytes 2359304 | tf_op jit(solution)/shard_map/ppermute | solution.py:20
  274.3 35.5 %collective-permute-start.39 = (bf16[768,512]{1,0:T(8,128)(2,1)S(1)}, bf16[768,512]{1,0:T(8,128)(2,1)S(1)}, u32[]{:S(2)}, u32[]{:S(2)}) collective-permute-start(bf16[768,512]{1,0:T(8,128)(2,1)S(1)} %add_convert_fusion.1), channel_id=1, source_target_pairs={{0,16},{4,20},{8,24},{12,28},{16,0},{20,4},{24,8},{28,12},{1,17},{... | collective-permute-start | bytes 2359304 | tf_op jit(solution)/shard_map/ppermute | solution.py:20
  (20 other events, 230.4 us)
